TPU v7x, 128 devices: a whole 4x4x4 slice. The times are simulated.
128 devices in a mesh: row: 16 (over z, y), col: 8 (over x, core).
Axes of the slice: x: 4, y: 4, z: 4, core: 2. Of those that a mesh axis runs over, the one named last changes fastest.
Arguments:
- covariance: float32 [4, 16, 256, 8, 8, 256], P(None, 'row', None, None, 'col'), as said below
- check_weights: float32 [4, 16, 256], P(None, 'row'), may hold values from 0.05 to 0.5
Outputs:
- trailing: float32 [4, 16, 256, 8, 8, 256], P(None, 'row', None, None, 'col')
- panels: float32 [4, 16, 256, 512], P(None, 'row')
- checksum: float32 [8, 8, 256], P(None, 'col')
Inputs may be any that keep to these rules, and one draw needn't show every extreme that they name: covariance is symmetric with smallest eigenvalue at least 0.5: an exponential kernel of jittered grid sites plus a nugget plus a small symmetric rough part.
All inputs are finite; a program needn't handle non-finite values.
Results may differ from a plain program's by a relative error of at most 0.0003.
Values sent between devices are 32-bit elements; how exact they have to be, the bound alone decides.
No kernel may reach another device: no remote copies, remote signals or barrier semaphores. Data moves between devices by JAX's collectives and lax.ppermute only.
A program may use at most 128 MiB of HBM per device.

v0:
```python
import jax
import jax.numpy as jnp
from jax import lax
from jax.sharding import PartitionSpec as P

HIGHEST = lax.Precision.HIGHEST


def from_root(value, axis, source):
    kept = jnp.where(lax.axis_index(axis) == source, value, 0).astype(value.dtype)
    return lax.psum(kept, axis)


def shards(covariance, check_weights):
    rows_size = lax.axis_size("row")
    cols_size = lax.axis_size("col")
    row_tiles = covariance.shape[0]
    width = covariance.shape[2]
    col_tiles = covariance.shape[3]
    matrix = covariance.reshape(row_tiles, width, col_tiles, width)
    row_index = lax.axis_index("row")
    col_index = lax.axis_index("col")
    global_rows = jnp.arange(row_tiles, dtype=jnp.int32) * rows_size + row_index
    global_cols = jnp.arange(col_tiles, dtype=jnp.int32) * cols_size + col_index
    panel_list = []
    for step in range(2):
        corner = matrix[step // rows_size, :, step // cols_size, :]
        corner = from_root(corner, "row", step % rows_size)
        corner = jnp.where(col_index == step % cols_size, corner, jnp.eye(width, dtype=jnp.float32))
        factor = jnp.linalg.cholesky(corner)
        column = matrix[:, :, step // cols_size, :].reshape(row_tiles * width, width)
        solved = jax.scipy.linalg.solve_triangular(factor, column.T, lower=True).T
        solved = solved.reshape(row_tiles, width, width)
        solved = jnp.where((global_rows >= step)[:, None, None], solved, 0.0)
        solved = from_root(solved, "col", step % cols_size)
        whole = lax.all_gather(solved, "row", axis=0, tiled=True)
        picked = global_cols % rows_size * row_tiles + global_cols // rows_size
        across = jnp.take(whole, picked, axis=0)
        matrix = matrix - jnp.einsum("iak,jbk->iajb", solved, across, precision=HIGHEST)
        panel_list.append(solved)
    keep = (global_rows >= 2)[:, None, None, None] & (global_cols >= 2)[None, None, :, None]
    trailing = jnp.where(keep, matrix, 0.0)
    weights = check_weights.reshape(row_tiles, width)
    partial_sums = jnp.einsum("ia,iajb->jb", weights, trailing, precision=HIGHEST)
    checksum = lax.psum(partial_sums, "row")
    panels = jnp.concatenate(panel_list, axis=2)
    return (
        trailing.reshape(row_tiles, 1, width, col_tiles, 1, width),
        panels.reshape(row_tiles, 1, width, 2 * width),
        checksum.reshape(col_tiles, 1, width),
    )


def solution(mesh):
    in_specs = (P(None, "row", None, None, "col", None), P(None, "row", None))
    out_specs = (
        P(None, "row", None, None, "col", None),
        P(None, "row", None, None),
        P(None, "col", None),
    )
    return jax.shard_map(shards, mesh=mesh, in_specs=in_specs, out_specs=out_specs, check_vma=False)
```

profile of v0, /device:TPU:0, one launch (start us, length us, event | category | flops | bytes accessed | tf_op | source)
XLA Modules:
  0.0 790.6 jit_solution(16580449472333877571)
XLA Ops:
  7.2 20.6 %copy.25 = f32[4,1,256,8,1,256]{2,5,3,0,4,1:T(8,128)} copy(f32[4,1,256,8,1,256]{5,4,3,2,1,0:T(1,128)} %param.7) | data formatting | bytes 16777216 | tf_op args[0]
  27.8 1.7 fusion.15
  29.5 1.3 slice.67
  31.5 85.0 %all-reduce.6.cloned.1.call-done = f32[256,256]{0,1:T(8,128)} async-done(((f32[256,256]{0,1:T(8,128)}), f32[256,256]{0,1:T(8,128)}) %all-reduce.6.cloned.1.call-update) | async-done | bytes 262160 | tf_op jit(solution)/shard_map/psum | solution.py:11
  116.6 1.0 convert_select_fusion.1
  117.7 1.0 fusion.17
  118.7 11.7 %cholesky.130 = f32[128,128]{1,0:T(8,128)S(1)} custom-call(f32[128,128]{1,0:T(8,128)S(1)} %cholesky.194), custom_call_target="Cholesky" | custom-call | tf_op jit(solution)/shard_map/jit(cholesky)/cholesky | solution.py:30
  130.4 9.8 %custom-call.13 = f32[1,128,128]{1,2,0:T(8,128)S(1)} custom-call(f32[1,128,128]{2,1,0:T(8,128)S(1)} %get-tuple-element.58), custom_call_target="InvertDiagBlocksLowerTriangular" | custom-call | tf_op jit(solution)/shard_map/jit(cholesky)/cholesky | solution.py:30
  140.8 11.7 %cholesky.147 = f32[128,128]{1,0:T(8,128)S(1)} custom-call(f32[128,128]{1,0:T(8,128)S(1)} %convolution_subtract_fusion.4), custom_call_target="Cholesky" | custom-call | tf_op jit(solution)/shard_map/jit(cholesky)/cholesky | solution.py:30
  152.5 0.7 compare_reduce_fusion.2
  154.7 4.6 while.4
  155.2 0.6 fusion.48
  155.8 1.4 bitcast_dynamic-update-slice_fusion.4
  157.3 0.6 fusion.48
  157.9 1.4 bitcast_dynamic-update-slice_fusion.4
  159.3 19.7 %custom-call.14 = f32[2,128,128]{1,2,0:T(8,128)S(1)} custom-call(f32[2,128,128]{2,1,0:T(8,128)S(1)} %get-tuple-element.20), custom_call_target="InvertDiagBlocksLowerTriangular" | custom-call | tf_op jit(solution)/shard_map/jit(_solve_triangular)/triangular_solve | solution.py:32
  179.0 0.6 fusion.12
  180.2 0.6 fusion.23
  181.3 1.2 select_select_fusion.1
  182.5 59.7 %all-reduce.8.cloned.1.call-done = f32[4,256,256]{2,1,0:T(8,128)} async-done(((f32[4,256,256]{2,1,0:T(8,128)}), f32[4,256,256]{2,1,0:T(8,128)}) %all-reduce.8.cloned.1.call-update) | async-done | bytes 1048592 | tf_op jit(solution)/shard_map/psum | solution.py:11
  242.4 113.1 %all-gather.3.cloned.1.call-done = f32[64,256,256]{2,1,0:T(8,128)} async-done(((f32[4,256,256]{2,1,0:T(8,128)}), f32[64,256,256]{2,1,0:T(8,128)}) %all-gather.3.cloned.1.call-update) | async-done | bytes 16777232 | tf_op jit(solution)/shard_map/all_gather | solution.py:36
  355.4 7.8 gather_fusion
  363.2 9.6 %convolution_subtract_fusion = f32[4,256,8,256]{1,3,2,0:T(8,128)S(1)} fusion(f32[8,256,256]{2,1,0:T(8,128)} %gather_fusion, f32[4,256,256]{2,1,0:T(8,128)S(1)} %copy-done.3, pred[8]{0:T(512)(128)(4,1)S(1)} %compare_and_fusion, f32[4,1,256,8,1,256]{2,5,3,0,4,1:T(8,128)} %copy.25), kind=kOutput, calls=%fused_computation.7 | convolution fusion | flops 6445072384 | bytes 19922952 | tf_op jit(solution)/shard_map/iak,jbk->iajb/dot_general | solution.py:39
  372.8 3.4 copy-done.2
  376.2 0.7 fusion.14
  377.2 1.0 slice-done
  378.8 82.3 %all-reduce.10.cloned.1.call-done = f32[256,256]{0,1:T(8,128)} async-done(((f32[256,256]{0,1:T(8,128)}), f32[256,256]{0,1:T(8,128)}) %all-reduce.10.cloned.1.call-update) | async-done | bytes 262160 | tf_op jit(solution)/shard_map/psum | solution.py:11
  461.4 11.7 %cholesky.164 = f32[128,128]{1,0:T(8,128)S(1)} custom-call(f32[128,128]{1,0:T(8,128)S(1)} %cholesky.197), custom_call_target="Cholesky" | custom-call | tf_op jit(solution)/shard_map/jit(cholesky)/cholesky | solution.py:30
  473.1 0.6 compare_reduce_fusion.1
  473.8 9.8 %custom-call.15 = f32[1,128,128]{1,2,0:T(8,128)S(1)} custom-call(f32[1,128,128]{2,1,0:T(8,128)S(1)} %get-tuple-element.54), custom_call_target="InvertDiagBlocksLowerTriangular" | custom-call | tf_op jit(solution)/shard_map/jit(cholesky)/cholesky | solution.py:30
  484.1 11.7 %cholesky.181 = f32[128,128]{1,0:T(8,128)S(1)} custom-call(f32[128,128]{1,0:T(8,128)S(1)} %convolution_subtract_fusion.3), custom_call_target="Cholesky" | custom-call | tf_op jit(solution)/shard_map/jit(cholesky)/cholesky | solution.py:30
  495.9 0.7 compare_reduce_fusion
  498.0 4.3 while.5
  498.2 0.6 fusion.49
  498.8 1.4 bitcast_dynamic-update-slice_fusion.5
  500.9 1.4 bitcast_dynamic-update-slice_fusion.5
  502.3 19.7 %custom-call.16 = f32[2,128,128]{1,2,0:T(8,128)S(1)} custom-call(f32[2,128,128]{2,1,0:T(8,128)S(1)} %get-tuple-element.21), custom_call_target="InvertDiagBlocksLowerTriangular" | custom-call | tf_op jit(solution)/shard_map/jit(_solve_triangular)/triangular_solve | solution.py:32
  522.0 0.6 fusion.10
  523.2 0.6 fusion.19
  524.3 1.2 select_select_fusion
  525.5 61.7 %all-reduce.12.cloned.1.call-done = f32[4,256,256]{2,1,0:T(8,128)} async-done(((f32[4,256,256]{2,1,0:T(8,128)}), f32[4,256,256]{2,1,0:T(8,128)}) %all-reduce.12.cloned.1.call-update) | async-done | bytes 1048592 | tf_op jit(solution)/shard_map/psum | solution.py:11
  587.3 2.8 maximum_bitcast_fusion
  590.1 109.9 %all-gather.5.cloned.1.call-done = f32[64,256,256]{2,1,0:T(8,128)} async-done(((f32[4,256,256]{2,1,0:T(8,128)}), f32[64,256,256]{2,1,0:T(8,128)}) %all-gather.5.cloned.1.call-update) | async-done | bytes 16777232 | tf_op jit(solution)/shard_map/all_gather | solution.py:36
  700.0 6.4 gather_fusion.1
  706.5 9.6 %subtract_select_fusion = f32[4,256,8,256]{1,3,2,0:T(8,128)S(1)} fusion(f32[4,256,8,256]{1,3,2,0:T(8,128)} %copy-done.2, pred[4,8]{1,0:T(4,128)(4,1)S(1)} %broadcast_and_fusion, f32[8,256,256]{2,1,0:T(8,128)S(1)} %gather_fusion.1, f32[4,256,256]{2,1,0:T(8,128)S(1)} %copy-done.4, pred[8]{0:T(512)(128)(4,1)S(1)} %compare_and_fusion), kind=kOutput, calls=%fused_computation.6 | convolution fusion | flops 6447169536 | bytes 19922984 | tf_op jit(solution)/shard_map/iak,jbk->iajb/dot_general | solution.py:39
  716.1 7.2 fusion.28
  723.3 39.5 %psum.39 = f32[8,1,256]{2,1,0:T(1,128)} all-reduce(f32[8,1,256]{2,1,0:T(1,128)S(1)} %reshape.113), channel_id=1, replica_groups=mesh['row'=16,'col'=8] {'row'}, use_global_device_ids=true, to_apply=%region_8.12 | all-reduce | flops 2048 | bytes 16384 | tf_op jit(solution)/shard_map/psum | solution.py:45
  762.9 20.5 %copy.36 = f32[4,1,256,8,1,256]{5,4,3,2,1,0:T(1,128)} copy(f32[4,1,256,8,1,256]{2,5,3,0,4,1:T(8,128)} %bitcast.106) | data formatting | bytes 16777216
  (69 shorter events, 6.3 us)
Async XLA Ops:
  7.2 708.9 %copy-start = (f32[4,1,256]{2,1,0:T(1,128)S(1)}, f32[4,1,256]{2,1,0:T(1,128)}, u32[]{:S(2)}) copy-start(f32[4,1,256]{2,1,0:T(1,128)} %param.8) | copy-start | bytes 12292
  7.2 109.4 %all-reduce.6.cloned.1.call-start = ((), (), s32[]{:S(2)}) async-start(), calls=%async_computation | async-start | bytes 524288 | tf_op jit(solution)/shard_map/psum | solution.py:11
  29.5 212.7 %all-reduce.8.cloned.1.call-start = ((), (), s32[]{:S(2)}) async-start(), calls=%async_computation.1 | async-start | bytes 2097152 | tf_op jit(solution)/shard_map/psum | solution.py:11
  182.5 173.0 %all-gather.3.cloned.1.call-start = ((), (), s32[]{:S(2)}) async-start(), calls=%async_computation.2 | async-start | bytes 17825792 | tf_op jit(solution)/shard_map/all_gather | solution.py:36
  242.2 218.9 %all-reduce.10.cloned.1.call-start = ((), (), s32[]{:S(2)}) async-start(), calls=%async_computation.3 | async-start | bytes 524288 | tf_op jit(solution)/shard_map/psum | solution.py:11
  242.4 120.8 %copy-start.3 = (f32[4,256,256]{2,1,0:T(8,128)S(1)}, f32[4,256,256]{2,1,0:T(8,128)}, u32[]{:S(2)}) copy-start(f32[4,256,256]{2,1,0:T(8,128)} %all-reduce.8.cloned.1.call-done) | copy-start | bytes 3145732
  372.8 3.4 copy-start.2
  376.9 1.2 slice-start
  377.0 210.2 %all-reduce.12.cloned.1.call-start = ((), (), s32[]{:S(2)}) async-start(), calls=%async_computation.4 | async-start | bytes 2097152 | tf_op jit(solution)/shard_map/psum | solution.py:11
  525.5 174.6 %all-gather.5.cloned.1.call-start = ((), (), s32[]{:S(2)}) async-start(), calls=%async_computation.5 | async-start | bytes 17825792 | tf_op jit(solution)/shard_map/all_gather | solution.py:36
  590.1 116.4 %copy-start.4 = (f32[4,256,256]{2,1,0:T(8,128)S(1)}, f32[4,256,256]{2,1,0:T(8,128)}, u32[]{:S(2)}) copy-start(f32[4,256,256]{2,1,0:T(8,128)} %all-reduce.12.cloned.1.call-done) | copy-start | bytes 3145732
  716.1 7.2 copy-start.1
Sparse Core Ops, SparseCore 0:
  29.6 86.9 all-reduce.5
  182.6 59.5 all-reduce.7
  244.6 110.7 all-gather.2
  377.1 84.0 all-reduce.9
  525.6 61.5 all-reduce.11
  589.2 110.7 all-gather.4
where the time goes:
time: 800 us; the launch traced here: 791 us
  waiting for transfers between devices  512 us (64%)
  other arithmetic  118 us (15%)
  local copies, waits for them, and re-layouts  71.5 us (9%)
  blocking collectives  39.5 us (5%)
  matrix products  31 us (4%)
  between operations  17.6 us (2%)
    psum x4, waiting for transfers between devices, from_root(): return lax.psum(kept, axis)  289 us
    all_gather x2, waiting for transfers between devices, shards(): whole = lax.all_gather(solved, 'row', axis=0, tiled=True)  223 us
    another operation x13, other arithmetic, shards(): factor = jnp.linalg.cholesky(corner)  68.7 us
    unnamed x12, local copies, waits for them, and re-layouts  44.5 us
    psum x1, blocking collectives, shards(): checksum = lax.psum(partial_sums, 'row')  39.5 us
    another operation x5, other arithmetic, shards(): solved = jax.scipy.linalg.solve_triangular(factor, column.T, lower=True).T  39.4 us
    dot_general x2, matrix products, shards(): jnp.einsum('iak,jbk->iajb', solved, across, precision=HIGHEST)  19.2 us
  transfers between devices with their start and end apart: 6, of which 6 were waited for; matrix products, arithmetic and copies ran while one was open for 1% of the time, Pallas kernels for 0%

commit v1 on v0

--- a/solution.py
+++ b/solution.py
@@ -33,7 +33,12 @@
         solved = solved.reshape(row_tiles, width, width)
         solved = jnp.where((global_rows >= step)[:, None, None], solved, 0.0)
         solved = from_root(solved, "col", step % cols_size)
-        whole = lax.all_gather(solved, "row", axis=0, tiled=True)
+        whole = jnp.concatenate(
+            lax.all_to_all(
+                jnp.stack([solved for _ in range(lax.axis_size("row"))], axis=0), "row", 0, 0
+            ),
+            axis=0,
+        )
         picked = global_cols % rows_size * row_tiles + global_cols // rows_size
         across = jnp.take(whole, picked, axis=0)
         matrix = matrix - jnp.einsum("iak,jbk->iajb", solved, across, precision=HIGHEST)

time: 800 us -> 1110 us (1.39)
  waiting for transfers between devices: 512 us -> 779 us
  local copies, waits for them, and re-layouts: 71.5 us -> 89.2 us
  starting transfers between devices: 0.42 us -> 14.9 us
    all_to_all x0 -> x2, waiting for transfers between devices: none -> 482 us  [shards(): lax.all_to_all(jnp.stack([solved for _ in range(lax.axis_size('row'))], a...]
    all_gather x2 -> x0, waiting for transfers between devices: 223 us -> none  [shards(): whole = lax.all_gather(solved, 'row', axis=0, tiled=True)]
    another operation x2, local copies, waits for them, and re-layouts: 0.66 us -> 18 us  [shards(): jnp.stack([solved for _ in range(lax.axis_size('row'))], axis=0)]
    all_to_all x0 -> x2, starting transfers between devices: none -> 14.6 us  [shards(): lax.all_to_all(jnp.stack([solved for _ in range(lax.axis_size('row'))], a...]
    unnamed x12 -> x10, local copies, waits for them, and re-layouts: 44.5 us -> 44.5 us
  transfers between devices with their start and end apart: 6 -> 6, of which waited for: 6 -> 6; matrix products, arithmetic and copies ran while one was open for 1% -> 0% of each run, Pallas kernels for 0% -> 0%
where the time goes in v1:
time: 1110 us; the launch traced here: 1090 us
  waiting for transfers between devices  779 us (70%)
  other arithmetic  117 us (11%)
  local copies, waits for them, and re-layouts  89.2 us (8%)
  blocking collectives  37.5 us (3%)
  matrix products  36.3 us (3%)
  between operations  17.1 us (2%)
  starting transfers between devices  14.9 us (1%)
    all_to_all x2, waiting for transfers between devices, shards(): lax.all_to_all(jnp.stack([solved for _ in range(lax.axis_size('row'))], a...  482 us
    psum x4, waiting for transfers between devices, from_root(): return lax.psum(kept, axis)  297 us
    another operation x13, other arithmetic, shards(): factor = jnp.linalg.cholesky(corner)  68.7 us
    unnamed x10, local copies, waits for them, and re-layouts  44.5 us
    another operation x5, other arithmetic, shards(): solved = jax.scipy.linalg.solve_triangular(factor, column.T, lower=True).T  39.4 us
    psum x1, blocking collectives, shards(): checksum = lax.psum(partial_sums, 'row')  37.5 us
  transfers between devices with their start and end apart: 6, of which 6 were waited for; matrix products, arithmetic and copies ran while one was open for 0% of the time, Pallas kernels for 0%

profile of v1, /device:TPU:0, one launch (start us, length us, event | category | flops | bytes accessed | tf_op | source)
XLA Modules:
  0.0 1091.5 jit_solution(9009056170017310148)
XLA Ops:
  7.2 20.6 %copy.14 = f32[4,1,256,8,1,256]{2,5,3,0,4,1:T(8,128)} copy(f32[4,1,256,8,1,256]{5,4,3,2,1,0:T(1,128)} %param.7) | data formatting | bytes 16777216 | tf_op args[0]
  27.8 1.7 fusion.15
  29.5 1.3 slice.67
  31.2 85.3 %all-reduce.6.cloned.1.call-done = f32[256,256]{0,1:T(8,128)} async-done(((f32[256,256]{0,1:T(8,128)}), f32[256,256]{0,1:T(8,128)}) %all-reduce.6.cloned.1.call-update) | async-done | bytes 262160 | tf_op jit(solution)/shard_map/psum | solution.py:11
  116.5 1.0 convert_select_fusion.1
  117.7 1.0 fusion.17
  118.7 11.7 %cholesky.130 = f32[128,128]{1,0:T(8,128)S(1)} custom-call(f32[128,128]{1,0:T(8,128)S(1)} %cholesky.194), custom_call_target="Cholesky" | custom-call | tf_op jit(solution)/shard_map/jit(cholesky)/cholesky | solution.py:30
  130.5 9.8 custom-call.13
  140.8 11.7 %cholesky.147 = f32[128,128]{1,0:T(8,128)S(1)} custom-call(f32[128,128]{1,0:T(8,128)S(1)} %convolution_subtract_fusion.4), custom_call_target="Cholesky" | custom-call | tf_op jit(solution)/shard_map/jit(cholesky)/cholesky | solution.py:30
  152.5 0.7 compare_reduce_fusion.2
  154.7 4.6 while.4
  155.9 1.4 bitcast_dynamic-update-slice_fusion.4
  157.9 1.4 bitcast_dynamic-update-slice_fusion.4
  159.3 19.7 %custom-call.14 = f32[2,128,128]{1,2,0:T(8,128)S(1)} custom-call(f32[2,128,128]{2,1,0:T(8,128)S(1)} %get-tuple-element.20), custom_call_target="InvertDiagBlocksLowerTriangular" | custom-call | tf_op jit(solution)/shard_map/jit(_solve_triangular)/triangular_solve | solution.py:32
  179.0 0.6 fusion.12
  179.7 1.0 convolution_subtract_fusion.2
  180.7 0.6 fusion.23
  181.8 1.2 select_select_fusion.1
  183.0 59.8 %all-reduce.8.cloned.1.call-done = f32[4,256,256]{2,1,0:T(8,128)} async-done(((f32[4,256,256]{2,1,0:T(8,128)}), f32[4,256,256]{2,1,0:T(8,128)}) %all-reduce.8.cloned.1.call-update) | async-done | bytes 1048592 | tf_op jit(solution)/shard_map/psum | solution.py:11
  242.7 9.0 stack.4
  251.7 7.2 all-to-all-start
  259.0 241.6 %all-to-all-done = f32[16,4,256,256]{3,2,1,0:T(8,128)} async-done(((f32[16,4,256,256]{3,2,1,0:T(8,128)}), f32[16,4,256,256]{3,2,1,0:T(8,128)}, u32[]{:S(2)}, u32[]{:S(2)}) %all-to-all-start) | async-done | bytes 16777248 | tf_op jit(solution)/shard_map/all_to_all | solution.py:37
  500.6 6.4 gather_fusion
  507.1 9.3 convolution_subtract_fusion
  516.4 3.4 copy-done.1
  519.8 0.7 fusion.14
  520.7 1.3 slice.69
  522.4 90.3 %all-reduce.10.cloned.1.call-done = f32[256,256]{0,1:T(8,128)} async-done(((f32[256,256]{0,1:T(8,128)}), f32[256,256]{0,1:T(8,128)}) %all-reduce.10.cloned.1.call-update) | async-done | bytes 262160 | tf_op jit(solution)/shard_map/psum | solution.py:11
  613.0 11.7 %cholesky.164 = f32[128,128]{1,0:T(8,128)S(1)} custom-call(f32[128,128]{1,0:T(8,128)S(1)} %cholesky.197), custom_call_target="Cholesky" | custom-call | tf_op jit(solution)/shard_map/jit(cholesky)/cholesky | solution.py:30
  624.8 9.8 custom-call.15
  635.1 11.7 %cholesky.181 = f32[128,128]{1,0:T(8,128)S(1)} custom-call(f32[128,128]{1,0:T(8,128)S(1)} %convolution_subtract_fusion.3), custom_call_target="Cholesky" | custom-call | tf_op jit(solution)/shard_map/jit(cholesky)/cholesky | solution.py:30
  647.4 0.7 compare_reduce_fusion
  649.6 4.3 while.5
  650.4 1.4 bitcast_dynamic-update-slice_fusion.5
  652.4 1.4 bitcast_dynamic-update-slice_fusion.5
  653.9 19.7 %custom-call.16 = f32[2,128,128]{1,2,0:T(8,128)S(1)} custom-call(f32[2,128,128]{2,1,0:T(8,128)S(1)} %get-tuple-element.21), custom_call_target="InvertDiagBlocksLowerTriangular" | custom-call | tf_op jit(solution)/shard_map/jit(_solve_triangular)/triangular_solve | solution.py:32
  674.2 1.0 convolution_subtract_fusion.1
  676.3 1.2 select_select_fusion
  677.5 61.7 %all-reduce.12.cloned.1.call-done = f32[4,256,256]{2,1,0:T(8,128)} async-done(((f32[4,256,256]{2,1,0:T(8,128)}), f32[4,256,256]{2,1,0:T(8,128)}) %all-reduce.12.cloned.1.call-update) | async-done | bytes 1048592 | tf_op jit(solution)/shard_map/psum | solution.py:11
  739.2 9.0 stack.5
  748.3 7.4 all-to-all-start.1
  755.8 1.6 maximum_bitcast_fusion
  757.4 240.0 %all-to-all-done.1 = f32[16,4,256,256]{3,2,1,0:T(8,128)} async-done(((f32[16,4,256,256]{3,2,1,0:T(8,128)}), f32[16,4,256,256]{3,2,1,0:T(8,128)}, u32[]{:S(2)}, u32[]{:S(2)}) %all-to-all-start.1) | async-done | bytes 16777248 | tf_op jit(solution)/shard_map/all_to_all | solution.py:37
  997.4 7.8 gather_fusion.1
  1005.2 12.1 %subtract_select_fusion = f32[4,256,8,256]{1,3,2,0:T(8,128)} fusion(f32[4,256,8,256]{1,3,2,0:T(8,128)} %copy-done.1, pred[4,8]{1,0:T(4,128)(4,1)S(1)} %broadcast_and_fusion, f32[8,256,256]{2,1,0:T(8,128)} %gather_fusion.1, f32[4,256,256]{2,1,0:T(8,128)S(1)} %copy-done.3, pred[8]{0:T(512)(128)(4,1)S(1)} %compare_and_fusion), kind=kOutput, calls=%fused_computation.6 | convolution fusion | flops 6447169536 | bytes 19922984 | tf_op jit(solution)/shard_map/iak,jbk->iajb/dot_general | solution.py:44
  1017.4 20.5 %copy.23 = f32[4,1,256,8,1,256]{5,4,3,2,1,0:T(1,128)} copy(f32[4,1,256,8,1,256]{2,5,3,0,4,1:T(8,128)} %bitcast.110) | data formatting | bytes 16777216
  1037.9 9.4 fusion.28
  1047.3 37.5 %psum.39 = f32[8,1,256]{2,1,0:T(1,128)} all-reduce(f32[8,1,256]{2,1,0:T(1,128)S(1)} %reshape.125), channel_id=1, replica_groups=mesh['row'=16,'col'=8] {'row'}, use_global_device_ids=true, to_apply=%region_8.12 | all-reduce | flops 2048 | bytes 16384 | tf_op jit(solution)/shard_map/psum | solution.py:50
  (64 shorter events, 8.1 us)
Async XLA Ops:
  7.2 1030.7 %copy-start = (f32[4,1,256]{2,1,0:T(1,128)S(1)}, f32[4,1,256]{2,1,0:T(1,128)}, u32[]{:S(2)}) copy-start(f32[4,1,256]{2,1,0:T(1,128)} %param.8) | copy-start | bytes 12292
  7.2 109.4 %all-reduce.6.cloned.1.call-start = ((), (), s32[]{:S(2)}) async-start(), calls=%async_computation.2 | async-start | bytes 524288 | tf_op jit(solution)/shard_map/psum | solution.py:11
  29.5 213.3 %all-reduce.8.cloned.1.call-start = ((), (), s32[]{:S(2)}) async-start(), calls=%async_computation.3 | async-start | bytes 2097152 | tf_op jit(solution)/shard_map/psum | solution.py:11
  251.7 255.3 %copy-start.2 = (f32[4,256,256]{2,1,0:T(8,128)S(1)}, f32[4,256,256]{2,1,0:T(8,128)}, u32[]{:S(2)}) copy-start(f32[4,256,256]{2,1,0:T(8,128)} %all-reduce.8.cloned.1.call-done) | copy-start | bytes 3145732
  251.7 248.8 %all-to-all-start = ((f32[16,4,256,256]{3,2,1,0:T(8,128)}), f32[16,4,256,256]{3,2,1,0:T(8,128)}, u32[]{:S(2)}, u32[]{:S(2)}) async-start(f32[16,4,256,256]{3,2,1,0:T(8,128)} %stack.4), calls=%async_computation | async-start | bytes 33554432 | tf_op jit(solution)/shard_map/all_to_all | solution.py:37
  258.9 353.8 %all-reduce.10.cloned.1.call-start = ((), (), s32[]{:S(2)}) async-start(), calls=%async_computation.4 | async-start | bytes 524288 | tf_op jit(solution)/shard_map/psum | solution.py:11
  516.4 3.4 copy-start.1
  520.5 218.7 %all-reduce.12.cloned.1.call-start = ((), (), s32[]{:S(2)}) async-start(), calls=%async_computation.5 | async-start | bytes 2097152 | tf_op jit(solution)/shard_map/psum | solution.py:11
  748.3 7.5 copy-start.3
  748.3 249.2 %all-to-all-start.1 = ((f32[16,4,256,256]{3,2,1,0:T(8,128)}), f32[16,4,256,256]{3,2,1,0:T(8,128)}, u32[]{:S(2)}, u32[]{:S(2)}) async-start(f32[16,4,256,256]{3,2,1,0:T(8,128)} %stack.5), calls=%async_computation.1 | async-start | bytes 33554432 | tf_op jit(solution)/shard_map/all_to_all | solution.py:37
Sparse Core Ops, SparseCore 0:
  29.6 86.9 all-reduce.5
  183.1 59.5 all-reduce.7
  520.6 92.0 all-reduce.9
  677.6 61.5 all-reduce.11
